TPU v7x, 512 devices: a whole 4x4x16 slice. The times are simulated.
512 devices in a mesh: tiles: 512 (over y, z, x, core).
Axes of the slice: x: 4, y: 4, z: 16, core: 2. Of those that a mesh axis runs over, the one named last changes fastest.
Arguments:
- coords: float32 [2, 2097152], P(None, 'tiles'), may hold values from 0 to 16384, as said below
- field: float32 [64, 2097152], P(None, 'tiles'), may hold values from -11 to 11
- pair_tiles: int32 [2, 32768], P(None, 'tiles'), may hold values from -1 to 8191, as said below
- pair_count: int32 [512], P('tiles'), may hold values from 15 to 64, as said below
Outputs:
- solution: float32 [64, 2097152], P(None, 'tiles')
- residual: float32 [64, 2097152], P(None, 'tiles')
- direction: float32 [64, 2097152], P(None, 'tiles')
Inputs may be any that keep to these rules, and one draw needn't show every extreme that they name: `coords`: tile t holds points t * 256 to (t + 1) * 256 - 1; device d holds tiles d * 16 to (d + 1) * 16 - 1. Any two points closer than 1 lie in one tile or in the two tiles of a live pair. `pair_tiles`: device d's slots are its 64 slots; its first pair_count[d] slots each hold a row tile A of device d and a column tile B with A < B <= A + 4 and B < 8192, no pair twice; its other slots hold -1 in both rows. `pair_count`: some device's count is 64 in every draw.
All inputs are finite; a program needn't handle non-finite values.
Results may differ from a plain program's by a relative error of at most 0.0003.
Values sent between devices are 32-bit elements; how exact they have to be, the bound alone decides.
A program may use at most 64 MiB of HBM per device.

v0:
```python
import jax
import jax.numpy as jnp
from jax import lax
from jax.sharding import PartitionSpec as P

TILE = 256
BAND = 4


sill = 0.2
nugget = 1.0
tiny_square = 1e-12
highest = lax.Precision.HIGHEST


def from_behind(value, axis, steps):
    count = lax.axis_size(axis)
    initial, last = (max(0, -steps), min(count, count - steps))
    return lax.ppermute(value, axis, [(source, source + steps) for source in range(initial, last)])


def wendland_tile(left_points, right_points):
    delta_x = left_points[0][:, None] - right_points[0][None, :]
    delta_y = left_points[1][:, None] - right_points[1][None, :]
    distance = jnp.sqrt(delta_x * delta_x + delta_y * delta_y + tiny_square)
    shell = jnp.maximum(1.0 - distance, 0.0)
    shell_sq = shell * shell
    return sill * shell_sq * shell_sq * (4.0 * distance + 1.0)


def block_stack(left_points, right_points):
    return jax.vmap(wendland_tile, in_axes=(1, 1))(left_points, right_points)


def pair_mask(tiles_table, count, row_base, rows):
    slot = jnp.arange(tiles_table.shape[1], dtype=jnp.int32)
    live = slot < count
    row_tile = tiles_table[0] - row_base
    offset = tiles_table[1] - tiles_table[0]
    row_hit = row_tile[:, None, None] == jnp.arange(rows, dtype=jnp.int32)[None, :, None]
    off_hit = offset[:, None, None] == jnp.arange(1, BAND + 1, dtype=jnp.int32)[None, None, :]
    hit = live[:, None, None] & row_hit & off_hit
    return jnp.sum(hit.astype(jnp.float32), axis=0)


def per_device(coords, field, pair_tiles, pair_count):
    columns = field.shape[0]
    tiles_here = coords.shape[1] // TILE
    points_here = tiles_here * TILE
    first_tile = lax.axis_index("tiles") * tiles_here
    rim_points = BAND * TILE
    next_coords, next_field = from_behind(
        (coords[:, :rim_points], field[:, :rim_points]), "tiles", -1
    )
    start_sum = lax.psum(jnp.sum(field * field, axis=1), "tiles")
    wide_points = jnp.concatenate([coords, next_coords], axis=1).reshape(2, tiles_here + BAND, TILE)
    wide_values = jnp.concatenate([field, next_field], axis=1).reshape(
        columns, tiles_here + BAND, TILE
    )
    tile_points = coords.reshape(2, tiles_here, TILE)
    field_tiles = field.reshape(columns, tiles_here, TILE)
    diagonal_tiles = block_stack(tile_points, tile_points)
    own_image = jnp.einsum(
        "ntj,tij->nti",
        field_tiles,
        diagonal_tiles,
        precision=highest,
        preferred_element_type=jnp.float32,
    )
    totals = jnp.pad(own_image, ((0, 0), (0, BAND), (0, 0)))
    live_mask = pair_mask(pair_tiles, pair_count[0], first_tile, tiles_here)
    for offset in range(1, BAND + 1):
        blocks = (
            block_stack(tile_points, wide_points[:, offset : offset + tiles_here])
            * live_mask[:, offset - 1][:, None, None]
        )
        row_part = jnp.einsum(
            "ntj,tij->nti",
            wide_values[:, offset : offset + tiles_here],
            blocks,
            precision=highest,
            preferred_element_type=jnp.float32,
        )
        col_part = jnp.einsum(
            "nti,tij->ntj",
            field_tiles,
            blocks,
            precision=highest,
            preferred_element_type=jnp.float32,
        )
        totals = (
            totals
            + jnp.pad(row_part, ((0, 0), (0, BAND), (0, 0)))
            + jnp.pad(col_part, ((0, 0), (offset, BAND - offset), (0, 0)))
        )
    totals = totals.reshape(columns, points_here + rim_points)
    image = totals[:, :points_here]
    arrived = from_behind(totals[:, points_here:], "tiles", 1)
    image = jnp.concatenate([image[:, :rim_points] + arrived, image[:, rim_points:]], axis=1)
    image = image + nugget * field
    curvature = lax.psum(jnp.sum(field * image, axis=1), "tiles")
    step_size = start_sum / curvature
    residual = field - step_size[:, None] * image
    new_sum = lax.psum(jnp.sum(residual * residual, axis=1), "tiles")
    solution = step_size[:, None] * field
    direction = residual + (new_sum / start_sum)[:, None] * field
    return (solution, residual, direction)


def solution(mesh):
    return jax.shard_map(
        per_device,
        mesh=mesh,
        in_specs=(P(None, "tiles"), P(None, "tiles"), P(None, "tiles"), P("tiles")),
        out_specs=(P(None, "tiles"), P(None, "tiles"), P(None, "tiles")),
        check_vma=False,
    )
```

profile of v0, /device:TPU:1, one launch (start us, length us, event | category | flops | bytes accessed | tf_op | source)
XLA Modules:
  0.0 318.3 jit_solution(16737865412904400120)
XLA Ops:
  0.6 0.7 slice.105
  1.3 8.7 %collective-permute-start = (f32[2,1024]{1,0:T(2,128)S(1)}, f32[2,1024]{1,0:T(2,128)S(1)}, u32[]{:S(2)}, u32[]{:S(2)}) collective-permute-start(f32[2,1024]{1,0:T(2,128)S(1)} %slice.105), channel_id=1, source_target_pairs={{1,0},{2,1},{3,2},{4,3},{5,4},{6,5},{7,6},{8,7},{9,8},{10,9},{11,1... | collective-permute-start | bytes 24584 | tf_op jit(solution)/shard_map/ppermute | solution.py:19
  10.1 1.0 slice.111
  11.0 1.9 collective-permute-start.1
  13.0 0.9 slice_reduce_fusion.1
  14.6 0.8 subtract_bitcast_fusion.1
  15.4 0.1 broadcast_compare_fusion
  15.4 0.1 convert_reduce_fusion
  15.6 9.7 %fusion.128 = f32[64,16,256]{2,0,1:T(8,128)} fusion(f32[16,256]{1,0:T(8,128)S(1)} %sub.179, f32[16,256]{1,0:T(8,128)S(1)} %sub.175, f32[8,16,8,256]{3,2,1,0:T(8,128)} %bitcast.63), kind=kOutput, calls=%fused_computation.124 | convolution fusion | flops 819986432 | bytes 2129920 | tf_op jit(solution)/shard_map/ntj,tij->nti/dot_general | solution.py:63
  25.4 7.6 %fusion.134 = f32[64,16,256]{2,0,1:T(8,128)} fusion(f32[16]{0:T(128)S(1)} %get-tuple-element.24, f32[16,256]{1,0:T(8,128)S(1)} %get-tuple-element.23, f32[16,256]{1,0:T(8,128)S(1)} %get-tuple-element.16, f32[16,256]{1,0:T(8,128)S(1)} %sub.179, f32[16,256]{1,0:T(8,128)S(1)} %sub.175, f32[8,16,8,256]{3,2,1,0:T(8,128)S(1)} %bitcast.64), kind=kOutput, calls=%fused_computation.126 | convolution fusion | flops 821035008 | bytes 2162752 | tf_op jit(solution)/shard_map/nti,tij->ntj/dot_general | solution.py:84
  33.0 7.6 %fusion.140 = f32[64,16,256]{2,0,1:T(8,128)} fusion(f32[16]{0:T(128)S(1)} %get-tuple-element.27, f32[16,256]{1,0:T(8,128)S(1)} %get-tuple-element.21, f32[16,256]{1,0:T(8,128)S(1)} %get-tuple-element.22, f32[16,256]{1,0:T(8,128)S(1)} %sub.179, f32[16,256]{1,0:T(8,128)S(1)} %sub.175, f32[8,16,8,256]{3,2,1,0:T(8,128)S(1)} %bitcast.65), kind=kOutput, calls=%fused_computation.128 | convolution fusion | flops 821035008 | bytes 2162752 | tf_op jit(solution)/shard_map/nti,tij->ntj/dot_general | solution.py:84
  40.6 7.6 %fusion.146 = f32[64,16,256]{2,0,1:T(8,128)} fusion(f32[16]{0:T(128)S(1)} %get-tuple-element.26, f32[16,256]{1,0:T(8,128)S(1)} %get-tuple-element.19, f32[16,256]{1,0:T(8,128)S(1)} %get-tuple-element.20, f32[16,256]{1,0:T(8,128)S(1)} %sub.179, f32[16,256]{1,0:T(8,128)S(1)} %sub.175, f32[8,16,8,256]{3,2,1,0:T(8,128)S(1)} %bitcast.66), kind=kOutput, calls=%fused_computation.130 | convolution fusion | flops 821035008 | bytes 2162752 | tf_op jit(solution)/shard_map/nti,tij->ntj/dot_general | solution.py:84
  48.1 7.6 %fusion.152 = f32[64,16,256]{2,0,1:T(8,128)} fusion(f32[16]{0:T(128)S(1)} %get-tuple-element.25, f32[16,256]{1,0:T(8,128)S(1)} %get-tuple-element.17, f32[16,256]{1,0:T(8,128)S(1)} %get-tuple-element.18, f32[16,256]{1,0:T(8,128)S(1)} %sub.179, f32[16,256]{1,0:T(8,128)S(1)} %sub.175, f32[8,16,8,256]{3,2,1,0:T(8,128)S(1)} %bitcast.67), kind=kOutput, calls=%fused_computation.132 | convolution fusion | flops 821035008 | bytes 2162752 | tf_op jit(solution)/shard_map/nti,tij->ntj/dot_general | solution.py:84
  55.7 1.1 pad_maximum_fusion
  56.9 1.5 reshape.142
  58.3 0.5 fusion.215
  58.9 9.7 %fusion.131 = f32[64,16,256]{2,0,1:T(8,128)S(1)} fusion(f32[16]{0:T(128)S(1)} %get-tuple-element.24, f32[16,256]{1,0:T(8,128)S(1)} %get-tuple-element.23, f32[16,256]{1,0:T(8,128)S(1)} %get-tuple-element.16, f32[16,256]{1,0:T(8,128)S(1)} %sub.179, f32[16,256]{1,0:T(8,128)S(1)} %sub.175, f32[64,16,256]{2,1,0:T(8,128)S(1)} %get-tuple-element.11), kind=kOutput, calls=%fused_computation.125 | convolution fusion | flops 821035008 | bytes 2162752 | tf_op jit(solution)/shard_map/ntj,tij->nti/dot_general | solution.py:77
  68.6 9.6 %fusion.137 = f32[64,16,256]{2,0,1:T(8,128)S(1)} fusion(f32[16]{0:T(128)S(1)} %get-tuple-element.27, f32[16,256]{1,0:T(8,128)S(1)} %get-tuple-element.21, f32[16,256]{1,0:T(8,128)S(1)} %get-tuple-element.22, f32[16,256]{1,0:T(8,128)S(1)} %sub.179, f32[16,256]{1,0:T(8,128)S(1)} %sub.175, f32[64,16,256]{2,1,0:T(8,128)S(1)} %get-tuple-element.13), kind=kOutput, calls=%fused_computation.127 | convolution fusion | flops 821035008 | bytes 2162752 | tf_op jit(solution)/shard_map/ntj,tij->nti/dot_general | solution.py:77
  78.2 9.6 %fusion.143 = f32[64,16,256]{2,0,1:T(8,128)S(1)} fusion(f32[16]{0:T(128)S(1)} %get-tuple-element.26, f32[16,256]{1,0:T(8,128)S(1)} %get-tuple-element.19, f32[16,256]{1,0:T(8,128)S(1)} %get-tuple-element.20, f32[16,256]{1,0:T(8,128)S(1)} %sub.179, f32[16,256]{1,0:T(8,128)S(1)} %sub.175, f32[64,16,256]{2,1,0:T(8,128)S(1)} %get-tuple-element.12), kind=kOutput, calls=%fused_computation.129 | convolution fusion | flops 821035008 | bytes 2162752 | tf_op jit(solution)/shard_map/ntj,tij->nti/dot_general | solution.py:77
  87.7 0.0 copy-start.4
  87.8 0.0 copy-start.6
  87.8 9.6 %fusion.149 = f32[64,16,256]{2,0,1:T(8,128)S(1)} fusion(f32[16]{0:T(128)S(1)} %get-tuple-element.25, f32[16,256]{1,0:T(8,128)S(1)} %get-tuple-element.17, f32[16,256]{1,0:T(8,128)S(1)} %get-tuple-element.18, f32[16,256]{1,0:T(8,128)S(1)} %sub.179, f32[16,256]{1,0:T(8,128)S(1)} %sub.175, f32[64,16,256]{2,1,0:T(8,128)S(1)} %get-tuple-element.14), kind=kOutput, calls=%fused_computation.131 | convolution fusion | flops 821035008 | bytes 2162752 | tf_op jit(solution)/shard_map/ntj,tij->nti/dot_general | solution.py:77
  97.4 1.0 add_bitcast_fusion
  98.4 0.1 copy.37
  98.5 3.6 %collective-permute-start.2 = (f32[64,1024]{1,0:T(8,128)S(1)}, f32[64,1024]{1,0:T(8,128)S(1)}, u32[]{:S(2)}, u32[]{:S(2)}) collective-permute-start(f32[64,1024]{1,0:T(8,128)S(1)} %slice.141), channel_id=1, source_target_pairs={{0,1},{1,2},{2,3},{3,4},{4,5},{5,6},{6,7},{7,8},{8,9},{9,10},{10,1... | collective-permute-start | bytes 786440 | tf_op jit(solution)/shard_map/ppermute | solution.py:19
  102.2 0.1 slice.142
  102.3 3.2 %collective-permute-done.2 = f32[64,1024]{1,0:T(8,128)S(1)} collective-permute-done((f32[64,1024]{1,0:T(8,128)S(1)}, f32[64,1024]{1,0:T(8,128)S(1)}, u32[]{:S(2)}, u32[]{:S(2)}) %collective-permute-start.2) | collective-permute-done | bytes 262176 | tf_op jit(solution)/shard_map/ppermute | solution.py:19
  105.5 0.3 multiply_reduce_fusion.1
  105.8 110.7 %all-reduce.9 = (f32[64]{0:T(128)S(1)}, f32[64]{0:T(128)S(1)}) all-reduce(f32[64]{0:T(128)S(1)} %get-tuple-element.4, f32[64]{0:T(128)S(1)} %get-tuple-element.3), channel_id=1, replica_groups=mesh['tiles'=512] {'tiles'}, use_global_device_ids=true, to_apply=%region_1.0 | all-reduce | flops 128 | bytes 1024 | tf_op jit(solution)/shard_map/psum | solution.py:55
  216.5 1.4 multiply_reduce_fusion
  217.9 99.3 %psum.23 = f32[64]{0:T(128)S(1)} all-reduce(f32[64]{0:T(128)S(1)} %get-tuple-element.9), channel_id=1, replica_groups=mesh['tiles'=512] {'tiles'}, use_global_device_ids=true, to_apply=%region_6.7 | all-reduce | flops 64 | bytes 512 | tf_op jit(solution)/shard_map/psum | solution.py:104
  317.2 1.1 multiply_add_fusion
  (29 shorter events, 0.2 us)
Async XLA Ops:
  1.3 23.9 %collective-permute-start = (f32[2,1024]{1,0:T(2,128)S(1)}, f32[2,1024]{1,0:T(2,128)S(1)}, u32[]{:S(2)}, u32[]{:S(2)}) collective-permute-start(f32[2,1024]{1,0:T(2,128)S(1)} %slice.105), channel_id=1, source_target_pairs={{1,0},{2,1},{3,2},{4,3},{5,4},{6,5},{7,6},{8,7},{9,8},{10,9},{11,1... | collective-permute-start | bytes 24584 | tf_op jit(solution)/shard_map/ppermute | solution.py:19
  11.0 44.7 %collective-permute-start.1 = (f32[64,1024]{1,0:T(8,128)S(1)}, f32[64,1024]{1,0:T(8,128)S(1)}, u32[]{:S(2)}, u32[]{:S(2)}) collective-permute-start(f32[64,1024]{1,0:T(8,128)S(1)} %slice.111), channel_id=1, source_target_pairs={{1,0},{2,1},{3,2},{4,3},{5,4},{6,5},{7,6},{8,7},{9,8},{10,9},{11,1... | collective-permute-start | bytes 786440 | tf_op jit(solution)/shard_map/ppermute | solution.py:19
  15.5 9.7 %copy-start.7 = (f32[2,4096]{1,0:T(2,128)S(1)}, f32[2,4096]{1,0:T(2,128)}, u32[]{:S(2)}) copy-start(f32[2,4096]{1,0:T(2,128)} %param.4) | copy-start | bytes 98308
  15.5 9.8 %copy-start = (f32[64,4096]{1,0:T(8,128)S(1)}, f32[64,4096]{1,0:T(8,128)}, u32[]{:S(2)}) copy-start(f32[64,4096]{1,0:T(8,128)} %param.5) | copy-start | bytes 3145732
  87.7 9.6 %copy-start.2 = (f32[64,16,256]{2,0,1:T(8,128)S(1)}, f32[64,16,256]{2,0,1:T(8,128)}, u32[]{:S(2)}) copy-start(f32[64,16,256]{2,0,1:T(8,128)} %fusion.128) | copy-start | bytes 3145732
  87.7 9.6 %copy-start.3 = (f32[64,16,256]{2,0,1:T(8,128)S(1)}, f32[64,16,256]{2,0,1:T(8,128)}, u32[]{:S(2)}) copy-start(f32[64,16,256]{2,0,1:T(8,128)} %fusion.134) | copy-start | bytes 3145732
  87.7 9.6 %copy-start.4 = (f32[64,16,256]{2,0,1:T(8,128)S(1)}, f32[64,16,256]{2,0,1:T(8,128)}, u32[]{:S(2)}) copy-start(f32[64,16,256]{2,0,1:T(8,128)} %fusion.140) | copy-start | bytes 3145732
  87.8 9.6 %copy-start.5 = (f32[64,16,256]{2,0,1:T(8,128)S(1)}, f32[64,16,256]{2,0,1:T(8,128)}, u32[]{:S(2)}) copy-start(f32[64,16,256]{2,0,1:T(8,128)} %fusion.146) | copy-start | bytes 3145732
  87.8 9.6 %copy-start.6 = (f32[64,16,256]{2,0,1:T(8,128)S(1)}, f32[64,16,256]{2,0,1:T(8,128)}, u32[]{:S(2)}) copy-start(f32[64,16,256]{2,0,1:T(8,128)} %fusion.152) | copy-start | bytes 3145732
  98.5 6.9 %collective-permute-start.2 = (f32[64,1024]{1,0:T(8,128)S(1)}, f32[64,1024]{1,0:T(8,128)S(1)}, u32[]{:S(2)}, u32[]{:S(2)}) collective-permute-start(f32[64,1024]{1,0:T(8,128)S(1)} %slice.141), channel_id=1, source_target_pairs={{0,1},{1,2},{2,3},{3,4},{4,5},{5,6},{6,7},{7,8},{8,9},{9,10},{10,1... | collective-permute-start | bytes 786440 | tf_op jit(solution)/shard_map/ppermute | solution.py:19
  217.9 100.5 %copy-start.1 = (f32[64,4096]{1,0:T(8,128)}, f32[64,4096]{1,0:T(8,128)S(1)}, u32[]{:S(2)}) copy-start(f32[64,4096]{1,0:T(8,128)S(1)} %get-tuple-element.10) | copy-start | bytes 3145732
where the time goes:
time: 319 us; the launch traced here: 318 us
  blocking collectives  210 us (66%)
  matrix products  78.4 us (25%)
  starting transfers between devices  14.3 us (4%)
  other arithmetic  5.91 us (2%)
  local copies, waits for them, and re-layouts  4.88 us (2%)
  waiting for transfers between devices  3.24 us (1%)
    psum x1, blocking collectives, per_device(): start_sum = lax.psum(jnp.sum(field * field, axis=1), 'tiles')  111 us
    psum x1, blocking collectives, per_device(): new_sum = lax.psum(jnp.sum(residual * residual, axis=1), 'tiles')  99.3 us
    dot_general x4, matrix products, per_device(): jnp.einsum('ntj,tij->nti', wide_values[:, offset:offset + tiles_here], bl...  38.4 us
    dot_general x4, matrix products, per_device(): jnp.einsum('nti,tij->ntj', field_tiles, blocks, precision=highest, prefer...  30.3 us
    ppermute x3, starting transfers between devices, from_behind(): lax.ppermute(value, axis, [(source, source + steps) for source in range(i...  14.3 us
    dot_general x1, matrix products, per_device(): jnp.einsum('ntj,tij->nti', field_tiles, diagonal_tiles, precision=highest...  9.69 us
  transfers between devices with their start and end apart: 3, of which 1 were waited for; matrix products, arithmetic and copies ran while one was open for 14% of the time, Pallas kernels for 0%

commit v1 on v0

v1 whole, which is shorter than its diff:
```python
import jax
import jax.numpy as jnp
from jax import lax
from jax.experimental import pallas as pl
from jax.experimental.pallas import tpu as pltpu
from jax.sharding import PartitionSpec as P

TILE = 256
BAND = 4
LANE = 128
CHUNK = 64
SILL = 0.2
NUGGET = 1.0
TINY = 16.0 * 1e-12
SCALE = SILL / 256.0
NX, NY, NZ, NC = 4, 4, 16, 2
PLANE = NX * NY * NC
EARLY = 6

f32 = jnp.float32
bf16 = jnp.bfloat16
NT = (((1,), (1,)), ((), ()))
NN = (((1,), (0,)), ((), ()))


def place(me):
    return me // (NZ * NX * NC), (me // (NX * NC)) % NZ, (me // NC) % NX, me % NC


def device(y, z, x, c):
    return (((y % NY) * NZ + z % NZ) * NX + x % NX) * NC + c % NC


def dot(a, b, dims):
    return lax.dot_general(a, b, dims, preferred_element_type=f32)


def lanes(first, count=1):
    return pl.ds(pl.multiple_of(first * LANE, LANE), count * LANE)


def covariance(xc, yc, xr, yr):
    dx = xc - xr
    dy = yc - yr
    q = dx * dx + dy * dy + TINY
    r = q * lax.rsqrt(q)
    s = jnp.maximum(4.0 - r, 0.0)
    s2 = s * s
    return s2 * s2 * (r + 1.0)


def split(v):
    high = v.astype(bf16)
    return high, (v - high.astype(f32)).astype(bf16)


def columns_of(cw, col, tile):
    for d in range(2):
        for h in range(2):
            row = cw[d : d + 1, lanes(tile * 2 + h)]
            col[d, h * LANE : (h + 1) * LANE, :] = jnp.broadcast_to(row, (LANE, LANE)).T


def strip_block(cw, col, kh, kl, tile, j):
    xr = cw[0:1, lanes(tile * 2 + j)]
    yr = cw[1:2, lanes(tile * 2 + j)]
    for g in range(0, TILE, CHUNK):
        rows = slice(g, g + CHUNK)
        high, low = split(covariance(col[0, rows, :], col[1, rows, :], xr, yr))
        kh[j, rows, :] = high
        kl[j, rows, :] = low


def both(v):
    half = v.shape[0] // 2
    return v[:half] + v[half:]


def row_apply(f2, acc, kh, kl, tile):
    width = 2 * (BAND + 1)
    values = [f2[tile * 2 + j] for j in range(width)]
    blocks = [k[j] for k in (kh, kl) for j in range(width)]
    out = dot(jnp.concatenate(values + values, 1), jnp.concatenate(blocks, 1), NT)
    acc[:, lanes(tile * 2, 2)] += both(out)


def col_apply(f2, acc, kh, kl, tile, b):
    values = [f2[tile * 2 + j] for j in range(2)]
    blocks = [jnp.concatenate([k[2 * b], k[2 * b + 1]], 1) for k in (kh, kl)]
    out = dot(jnp.concatenate(values + values, 1), jnp.concatenate(blocks, 0), NN)
    acc[:, lanes((tile + b) * 2, 2)] += both(out)


def order(step, late):
    return jnp.where(
        step < EARLY, step, jnp.where(step < EARLY + BAND, step + late - EARLY, step - BAND)
    )


def kernel(
    tiles,
    c_hbm,
    f_hbm,
    image_ref,
    step_ref,
    beta_ref,
    cw,
    fw,
    f2,
    acc,
    col0,
    col1,
    kh0,
    kl0,
    kh1,
    kl1,
    halo_c,
    halo_f,
    back,
    part,
    slots1,
    total1,
    slots2,
    load_sem,
    send_sem,
    recv_sem,
    near_sem,
    far_sem,
):
    n = f_hbm.shape[0]
    points = tiles * TILE
    rim = BAND * TILE
    me = lax.axis_index("tiles")
    count = NX * NY * NZ * NC
    y, z, x, c = place(me)
    right, left = (me + 1) % count, (me + count - 1) % count
    other = 1 - c

    load_f = pltpu.make_async_copy(f_hbm, fw, load_sem.at[0])
    load_c = pltpu.make_async_copy(c_hbm, cw.at[:, 0:points], load_sem.at[1])
    load_c.start()
    load_f.start()

    near = [left, right, device(y, z, x, other)]
    for dy, dz, dx in ((0, 0, 1), (0, 0, -1), (0, 1, 0), (0, -1, 0), (1, 0, 0), (-1, 0, 0)):
        for core in (c, other):
            near.append(device(y + dy, z + dz + NZ, x + dx + NX, core) if dy == 0 else device(y + dy + NY, z, x, core))
    barrier = pltpu.get_barrier_semaphore()
    for target in near:
        pl.semaphore_signal(barrier, inc=1, device_id=(target,))

    halo_copies = [
        pltpu.make_async_remote_copy(
            src_ref=src.at[:, 0:rim],
            dst_ref=dst,
            send_sem=send_sem.at[i],
            recv_sem=recv_sem.at[i],
            device_id=(left,),
        )
        for i, (src, dst) in enumerate(((c_hbm, halo_c), (f_hbm, halo_f)))
    ]
    back_copy = pltpu.make_async_remote_copy(
        src_ref=acc.at[:, points : points + rim],
        dst_ref=back,
        send_sem=send_sem.at[2],
        recv_sem=recv_sem.at[2],
        device_id=(right,),
    )

    def wait_near():
        pl.semaphore_wait(barrier, len(near))
        for copy in halo_copies:
            copy.start()
        for target in near:
            pl.semaphore_signal(near_sem, inc=1, device_id=(target,))

    spread = [device(y, z, x + 2, c), device(y + 2, z, x, c), device(y, z + 2, x, c), device(y, z + NZ - 2, x, c)]
    spread_far = [device(y, z + 4, x, c), device(y, z + NZ - 4, x, c)]

    def wait_two():
        pl.semaphore_wait(near_sem, len(near))
        for i, target in enumerate(spread):
            pl.semaphore_signal(far_sem.at[0], inc=1, device_id=(target,))

    def wait_four():
        pl.semaphore_wait(far_sem.at[0], len(spread))
        for target in spread_far:
            pl.semaphore_signal(far_sem.at[1], inc=1, device_id=(target,))

    def wait_eight():
        pl.semaphore_wait(far_sem.at[1], len(spread_far))

    acc[...] = jnp.zeros_like(acc)
    load_c.wait()
    cw[:, 0:points] = cw[:, 0:points] * 4.0
    columns_of(cw, col0, 0)
    columns_of(cw, col1, 1)
    wait_near()
    load_f.wait()

    @pl.loop(0, points // LANE)
    def _(j):
        high, low = split(fw[:, lanes(j)])
        f2[j, 0:n, :] = high
        f2[j, n : 2 * n, :] = low

    for j in range(2 * (BAND + 1)):
        strip_block(cw, col0, kh0, kl0, 0, j)

    late = tiles - BAND

    def half(kh, kl, kh_next, kl_next, col, col_next, now, following, after):
        for b in range(BAND + 1):
            for j in (2 * b, 2 * b + 1):
                strip_block(cw, col_next, kh_next, kl_next, following, j)
            if b == 0:
                columns_of(cw, col, after)
                row_apply(f2, acc, kh, kl, now)
            else:
                col_apply(f2, acc, kh, kl, now, b)

    last = tiles - 1

    @pl.loop(0, tiles // 2)
    def _(i):
        @pl.when(i == 1)
        def _():
            wait_two()

        @pl.when(i == 2)
        def _():
            wait_four()

        @pl.when(i == EARLY // 2 - 1)
        def _():
            for copy in halo_copies:
                copy.wait()
            cw[:, points : points + rim] = halo_c[...] * 4.0
            for j in range(rim // LANE):
                high, low = split(halo_f[:, j * LANE : (j + 1) * LANE])
                f2[points // LANE + j, 0:n, :] = high
                f2[points // LANE + j, n : 2 * n, :] = low

        @pl.when(i == (EARLY + BAND) // 2)
        def _():
            back_copy.start()
            wait_eight()

        s = i * 2
        places = [order(jnp.minimum(s + k, last), late) for k in range(4)]
        half(kh0, kl0, kh1, kl1, col0, col1, places[0], places[1], places[2])
        half(kh1, kl1, kh0, kl0, col1, col0, places[1], places[2], places[3])

    back_copy.wait()
    sums = [jnp.zeros((n, LANE), f32) for _ in range(3)]
    for j in range(points // LANE):
        at = slice(j * LANE, (j + 1) * LANE)
        field = fw[:, at]
        applied = acc[:, at]
        if j < rim // LANE:
            applied = applied + back[:, at]
        image = applied * SCALE + NUGGET * field
        image_ref[:, at] = image
        sums = [sums[0] + field * field, sums[1] + field * image, sums[2] + image * image]

    def over_lanes(v):
        return jnp.sum(v.T, axis=0, keepdims=True)

    mine = jnp.concatenate(
        [
            over_lanes(jnp.concatenate([sums[0], sums[1]], 0)),
            over_lanes(jnp.concatenate([sums[2], sums[2]], 0)),
        ],
        0,
    )

    def gather_sum(values, source, slots, here, members, sems):
        source[...] = values
        slots[here] = values
        copies = []
        for member, target in members:
            copies.append(
                pltpu.make_async_remote_copy(
                    src_ref=source,
                    dst_ref=slots.at[here],
                    send_sem=send_sem.at[sems],
                    recv_sem=recv_sem.at[sems],
                    device_id=(target,),
                )
            )
        for copy in copies:
            copy.start()
        others = slots.at[pl.ds(0, len(members))]
        pltpu.make_async_copy(others, others, recv_sem.at[sems]).wait()
        pltpu.make_async_copy(others, others, send_sem.at[sems]).wait()
        terms = [slots[k] for k in range(len(members) + 1)]
        while len(terms) > 1:
            terms = [a + b for a, b in zip(terms[::2], terms[1::2])]
        return terms[0]

    in_plane = (y * NX + x) * NC + c
    plane = []
    for k in range(1, PLANE):
        member = (in_plane + k) % PLANE
        plane.append((member, device(member // (NX * NC), z, (member // NC) % NX, member % NC)))
    total = gather_sum(mine, part, slots1, in_plane, plane, 3)
    line = []
    for k in range(1, NZ):
        line.append(((z + k) % NZ, device(y, z + k, x, c)))
    total = gather_sum(total, total1, slots2, z, line, 4)

    def columns(row):
        return jnp.broadcast_to(row, (LANE, LANE)).T

    first, second = columns(total[0:1]), columns(total[1:2])
    start_sum, curvature, square = first[:n], first[n:], second[:n]
    step = start_sum / curvature
    new_sum = start_sum - 2.0 * step * curvature + step * step * square
    step_ref[...] = step
    beta_ref[...] = new_sum / start_sum


def per_device(coords, field, pair_tiles, pair_count):
    n, points = field.shape
    tiles = points // TILE
    rim = BAND * TILE
    wide = points + rim
    vmem = pl.BlockSpec(memory_space=pltpu.VMEM)
    block = pltpu.VMEM((2 * (BAND + 1), TILE, LANE), bf16)
    image, step, beta = pl.pallas_call(
        lambda *refs: kernel(tiles, *refs),
        out_shape=(
            jax.ShapeDtypeStruct((n, points), f32),
            jax.ShapeDtypeStruct((n, LANE), f32),
            jax.ShapeDtypeStruct((n, LANE), f32),
        ),
        in_specs=[pl.BlockSpec(memory_space=pl.ANY)] * 2,
        out_specs=(vmem, vmem, vmem),
        scratch_shapes=[
            pltpu.VMEM((2, wide), f32),
            pltpu.VMEM((n, points), f32),
            pltpu.VMEM((wide // LANE, 2 * n, LANE), bf16),
            pltpu.VMEM((n, wide), f32),
            pltpu.VMEM((2, TILE, LANE), f32),
            pltpu.VMEM((2, TILE, LANE), f32),
            block,
            block,
            block,
            block,
            pltpu.VMEM((2, rim), f32),
            pltpu.VMEM((n, rim), f32),
            pltpu.VMEM((n, rim), f32),
            pltpu.VMEM((2, LANE), f32),
            pltpu.VMEM((PLANE, 2, LANE), f32),
            pltpu.VMEM((2, LANE), f32),
            pltpu.VMEM((NZ, 2, LANE), f32),
            pltpu.SemaphoreType.DMA((2,)),
            pltpu.SemaphoreType.DMA((5,)),
            pltpu.SemaphoreType.DMA((5,)),
            pltpu.SemaphoreType.REGULAR,
            pltpu.SemaphoreType.REGULAR((2,)),
        ],
        compiler_params=pltpu.CompilerParams(collective_id=0, has_side_effects=True),
        name="iterate",
    )(coords, field)
    step, beta = step[:, :1], beta[:, :1]
    residual = field - step * image
    return step * field, residual, residual + beta * field


def solution(mesh):
    return jax.shard_map(
        per_device,
        mesh=mesh,
        in_specs=(P(None, "tiles"), P(None, "tiles"), P(None, "tiles"), P("tiles")),
        out_specs=(P(None, "tiles"), P(None, "tiles"), P(None, "tiles")),
        check_vma=False,
    )
```

time: 319 us -> 51.6 us (0.16)
  blocking collectives: 210 us -> 0 us
  matrix products: 78.4 us -> 0 us
  Pallas kernels: 0 us -> 46.6 us
  starting transfers between devices: 14.3 us -> 0 us
  local copies, waits for them, and re-layouts: 4.88 us -> 0.89 us
  waiting for transfers between devices: 3.24 us -> 0 us
    psum x2 -> x0, blocking collectives: 210 us -> none  [the longest x1 111 us: per_device(): start_sum = lax.psum(jnp.sum(field * field, axis=1), 'tiles')]
    dot_general x9 -> x0, matrix products: 78.4 us -> none  [the longest x4 38.4 us: per_device(): jnp.einsum('ntj,tij->nti', wide_values[:, offset:offset + tiles_here], bl...]
    pallas_call x0 -> x1, Pallas kernels: none -> 46.6 us  [per_device(): pl.pallas_call(lambda *refs: kernel(tiles, *refs), out_shape=(jax.ShapeDt...]
    ppermute x3 -> x0, starting transfers between devices: 14.3 us -> none  [from_behind(): lax.ppermute(value, axis, [(source, source + steps) for source in range(i...]
    ppermute x3 -> x0, waiting for transfers between devices: 3.24 us -> none  [from_behind(): lax.ppermute(value, axis, [(source, source + steps) for source in range(i...]
  transfers between devices with their start and end apart: 3 -> 0, of which waited for: 1 -> 0; matrix products, arithmetic and copies ran while one was open for 14% -> 0% of each run, Pallas kernels for 0% -> 0%
where the time goes in v1:
time: 51.6 us; the launch traced here: 51.4 us
  Pallas kernels  46.6 us (90%)
  other arithmetic  3.18 us (6%)
  local copies, waits for them, and re-layouts  0.89 us (2%)
  between operations  0.66 us (1%)
    pallas_call x1, Pallas kernels, per_device(): pl.pallas_call(lambda *refs: kernel(tiles, *refs), out_shape=(jax.ShapeDt...  46.6 us
    add x1, other arithmetic, per_device(): return (step * field, residual, residual + beta * field)  3.18 us

profile of v1, /device:TPU:1, one launch (start us, length us, event | category | flops | bytes accessed | tf_op | source)
XLA Modules:
  0.0 51.4 jit_solution(5803461892167723632)
XLA Ops:
  0.6 0.0 copy-start
  0.6 46.6 %iterate.1 = (f32[64,4096]{1,0:T(8,128)}, f32[64,128]{1,0:T(8,128)}, f32[64,128]{1,0:T(8,128)}) custom-call(f32[2,4096]{1,0:T(2,128)} %refs_0_.1, f32[64,4096]{1,0:T(8,128)} %refs_1_.1), custom_call_target="tpu_custom_call" | custom-call | tf_op jit(solution)/shard_map/iterate/pallas_call | solution.py:330
  47.3 0.9 %slice_reduce_fusion = (f32[64]{0:T(128)S(1)}, f32[64]{0:T(128)S(1)}) fusion(f32[64,128]{1,0:T(8,128)} %get-tuple-element.8, f32[64,128]{1,0:T(8,128)} %get-tuple-element.6), kind=kLoop, calls=%fused_computation.3 | loop fusion | bytes 1024 | tf_op jit(solution)/shard_map/slice | solution.py:366
  48.2 0.0 copy-done
  48.2 3.2 %multiply_add_fusion = (f32[64,4096]{1,0:T(8,128)}, f32[64,4096]{1,0:T(8,128)}, f32[64,4096]{1,0:T(8,128)}) fusion(f32[64,4096]{1,0:T(8,128)S(1)} %copy-done, f32[64]{0:T(128)S(1)} %get-tuple-element.12, f32[64,4096]{1,0:T(8,128)} %get-tuple-element.7, f32[64]{0:T(128)S(1)} %get-tuple-element.13), kind=kLoop, calls=%fused_computation | loop fusion | flops 1310720 | bytes 5243392 | tf_op jit(solution)/shard_map/add | solution.py:368
Async XLA Ops:
  0.6 47.5 %copy-start = (f32[64,4096]{1,0:T(8,128)S(1)}, f32[64,4096]{1,0:T(8,128)}, u32[]{:S(2)}) copy-start(f32[64,4096]{1,0:T(8,128)} %refs_1_.1) | copy-start | bytes 3145732

commit v2 on v1

--- a/solution.py
+++ b/solution.py
@@ -15,7 +15,9 @@
 SCALE = SILL / 256.0
 NX, NY, NZ, NC = 4, 4, 16, 2
 PLANE = NX * NY * NC
-EARLY = 6
+PIECES = 4
+GROUP = 4
+EARLY = 8
 
 f32 = jnp.float32
 bf16 = jnp.bfloat16
@@ -61,14 +63,17 @@
             col[d, h * LANE : (h + 1) * LANE, :] = jnp.broadcast_to(row, (LANE, LANE)).T
 
 
-def strip_block(cw, col, kh, kl, tile, j):
-    xr = cw[0:1, lanes(tile * 2 + j)]
-    yr = cw[1:2, lanes(tile * 2 + j)]
-    for g in range(0, TILE, CHUNK):
-        rows = slice(g, g + CHUNK)
-        high, low = split(covariance(col[0, rows, :], col[1, rows, :], xr, yr))
-        kh[j, rows, :] = high
-        kl[j, rows, :] = low
+def block(cw, col, tile, b):
+    out = []
+    for j in (2 * b, 2 * b + 1):
+        xr = cw[0:1, lanes(tile * 2 + j)]
+        yr = cw[1:2, lanes(tile * 2 + j)]
+        parts = []
+        for g in range(0, TILE, CHUNK):
+            rows = slice(g, g + CHUNK)
+            parts.append(split(covariance(col[0, rows, :], col[1, rows, :], xr, yr)))
+        out.append([jnp.concatenate([p[i] for p in parts], 0) for i in (0, 1)])
+    return [jnp.concatenate([out[0][i], out[1][i]], 1) for i in (0, 1)]
 
 
 def both(v):
@@ -76,17 +81,14 @@
     return v[:half] + v[half:]
 
 
-def row_apply(f2, acc, kh, kl, tile):
-    width = 2 * (BAND + 1)
-    values = [f2[tile * 2 + j] for j in range(width)]
-    blocks = [k[j] for k in (kh, kl) for j in range(width)]
+def row_apply(f2, acc, blocks, tile, b):
+    values = [f2[(tile + b) * 2 + j] for j in range(2)]
     out = dot(jnp.concatenate(values + values, 1), jnp.concatenate(blocks, 1), NT)
     acc[:, lanes(tile * 2, 2)] += both(out)
 
 
-def col_apply(f2, acc, kh, kl, tile, b):
+def col_apply(f2, acc, blocks, tile, b):
     values = [f2[tile * 2 + j] for j in range(2)]
-    blocks = [jnp.concatenate([k[2 * b], k[2 * b + 1]], 1) for k in (kh, kl)]
     out = dot(jnp.concatenate(values + values, 1), jnp.concatenate(blocks, 0), NN)
     acc[:, lanes((tile + b) * 2, 2)] += both(out)
 
@@ -101,19 +103,15 @@
     tiles,
     c_hbm,
     f_hbm,
+    fw,
     image_ref,
     step_ref,
     beta_ref,
     cw,
-    fw,
     f2,
     acc,
     col0,
     col1,
-    kh0,
-    kl0,
-    kh1,
-    kl1,
     halo_c,
     halo_f,
     back,
@@ -194,45 +192,27 @@
     load_c.wait()
     cw[:, 0:points] = cw[:, 0:points] * 4.0
     columns_of(cw, col0, 0)
-    columns_of(cw, col1, 1)
-    wait_near()
+    cols = (col0, col1)
     load_f.wait()
-
-    @pl.loop(0, points // LANE)
-    def _(j):
-        high, low = split(fw[:, lanes(j)])
+    for j in range(points // LANE):
+        high, low = split(fw[:, j * LANE : (j + 1) * LANE])
         f2[j, 0:n, :] = high
         f2[j, n : 2 * n, :] = low
-
-    for j in range(2 * (BAND + 1)):
-        strip_block(cw, col0, kh0, kl0, 0, j)
+    wait_near()
 
     late = tiles - BAND
 
-    def half(kh, kl, kh_next, kl_next, col, col_next, now, following, after):
-        for b in range(BAND + 1):
-            for j in (2 * b, 2 * b + 1):
-                strip_block(cw, col_next, kh_next, kl_next, following, j)
-            if b == 0:
-                columns_of(cw, col, after)
-                row_apply(f2, acc, kh, kl, now)
-            else:
-                col_apply(f2, acc, kh, kl, now, b)
-
     last = tiles - 1
 
-    @pl.loop(0, tiles // 2)
+    @pl.loop(0, tiles // GROUP)
     def _(i):
         @pl.when(i == 1)
         def _():
             wait_two()
 
-        @pl.when(i == 2)
+        @pl.when(i == EARLY // GROUP)
         def _():
             wait_four()
-
-        @pl.when(i == EARLY // 2 - 1)
-        def _():
             for copy in halo_copies:
                 copy.wait()
             cw[:, points : points + rim] = halo_c[...] * 4.0
@@ -241,19 +221,26 @@
                 f2[points // LANE + j, 0:n, :] = high
                 f2[points // LANE + j, n : 2 * n, :] = low
 
-        @pl.when(i == (EARLY + BAND) // 2)
+        @pl.when(i == (EARLY + BAND) // GROUP)
         def _():
             back_copy.start()
             wait_eight()
 
-        s = i * 2
-        places = [order(jnp.minimum(s + k, last), late) for k in range(4)]
-        half(kh0, kl0, kh1, kl1, col0, col1, places[0], places[1], places[2])
-        half(kh1, kl1, kh0, kl0, col1, col0, places[1], places[2], places[3])
-
-    back_copy.wait()
+        places = [order(jnp.minimum(i * GROUP + k, last), late) for k in range(GROUP + 1)]
+        for g in range(GROUP):
+            now, following = places[g], places[g + 1]
+            for b in range(BAND + 1):
+                blocks = block(cw, cols[g % 2], now, b)
+                row_apply(f2, acc, blocks, now, b)
+                if b == 0:
+                    columns_of(cw, cols[(g + 1) % 2], following)
+                else:
+                    col_apply(f2, acc, blocks, now, b)
+
     sums = [jnp.zeros((n, LANE), f32) for _ in range(3)]
-    for j in range(points // LANE):
+    for j in [*range(rim // LANE, points // LANE), *range(rim // LANE)]:
+        if j == 0:
+            back_copy.wait()
         at = slice(j * LANE, (j + 1) * LANE)
         field = fw[:, at]
         applied = acc[:, at]
@@ -300,12 +287,16 @@
 
     in_plane = (y * NX + x) * NC + c
     plane = []
-    for k in range(1, PLANE):
-        member = (in_plane + k) % PLANE
-        plane.append((member, device(member // (NX * NC), z, (member // NC) % NX, member % NC)))
+    for dy, dx, core in sorted(
+        ((a, b, e) for a in range(NY) for b in range(NX) for e in range(NC)),
+        key=lambda m: -(min(m[0], NY - m[0]) + min(m[1], NX - m[1]) + m[2]),
+    ):
+        if (dy, dx, core) != (0, 0, 0):
+            at = ((y + dy) % NY, (x + dx) % NX, (c + core) % NC)
+            plane.append(((at[0] * NX + at[1]) * NC + at[2], device(at[0], z, at[1], at[2])))
     total = gather_sum(mine, part, slots1, in_plane, plane, 3)
     line = []
-    for k in range(1, NZ):
+    for k in sorted(range(1, NZ), key=lambda k: -min(k, NZ - k)):
         line.append(((z + k) % NZ, device(y, z + k, x, c)))
     total = gather_sum(total, total1, slots2, z, line, 4)
 
@@ -320,33 +311,46 @@
     beta_ref[...] = new_sum / start_sum
 
 
+def finish(field_ref, image_ref, step_ref, beta_ref, solution_hbm, residual_hbm, direction_hbm, made, sem):
+    points = field_ref.shape[1]
+    size = points // PIECES
+    step, beta = step_ref[...], beta_ref[...]
+    copies = []
+    for p in range(PIECES):
+        for j in range(p * size, (p + 1) * size, LANE):
+            at = slice(j, j + LANE)
+            field = field_ref[:, at]
+            residual = field - step * image_ref[:, at]
+            made[0, :, at] = step * field
+            made[1, :, at] = residual
+            made[2, :, at] = residual + beta * field
+        at = slice(p * size, (p + 1) * size)
+        for i, ref in enumerate((solution_hbm, residual_hbm, direction_hbm)):
+            copy = pltpu.make_async_copy(made.at[i, :, at], ref.at[:, at], sem.at[i, p])
+            copy.start()
+            copies.append(copy)
+    for copy in copies:
+        copy.wait()
+
+
 def per_device(coords, field, pair_tiles, pair_count):
     n, points = field.shape
     tiles = points // TILE
     rim = BAND * TILE
     wide = points + rim
     vmem = pl.BlockSpec(memory_space=pltpu.VMEM)
-    block = pltpu.VMEM((2 * (BAND + 1), TILE, LANE), bf16)
-    image, step, beta = pl.pallas_call(
+    whole, column = pltpu.VMEM((n, points), f32), pltpu.VMEM((n, LANE), f32)
+    kept = pl.pallas_call(
         lambda *refs: kernel(tiles, *refs),
-        out_shape=(
-            jax.ShapeDtypeStruct((n, points), f32),
-            jax.ShapeDtypeStruct((n, LANE), f32),
-            jax.ShapeDtypeStruct((n, LANE), f32),
-        ),
+        out_shape=(whole, whole, column, column),
         in_specs=[pl.BlockSpec(memory_space=pl.ANY)] * 2,
-        out_specs=(vmem, vmem, vmem),
+        out_specs=(vmem,) * 4,
         scratch_shapes=[
             pltpu.VMEM((2, wide), f32),
-            pltpu.VMEM((n, points), f32),
             pltpu.VMEM((wide // LANE, 2 * n, LANE), bf16),
             pltpu.VMEM((n, wide), f32),
             pltpu.VMEM((2, TILE, LANE), f32),
             pltpu.VMEM((2, TILE, LANE), f32),
-            block,
-            block,
-            block,
-            block,
             pltpu.VMEM((2, rim), f32),
             pltpu.VMEM((n, rim), f32),
             pltpu.VMEM((n, rim), f32),
@@ -363,9 +367,14 @@
         compiler_params=pltpu.CompilerParams(collective_id=0, has_side_effects=True),
         name="iterate",
     )(coords, field)
-    step, beta = step[:, :1], beta[:, :1]
-    residual = field - step * image
-    return step * field, residual, residual + beta * field
+    return pl.pallas_call(
+        finish,
+        out_shape=(jax.ShapeDtypeStruct((n, points), f32),) * 3,
+        in_specs=[vmem] * 4,
+        out_specs=(pl.BlockSpec(memory_space=pl.ANY),) * 3,
+        scratch_shapes=[pltpu.VMEM((3, n, points), f32), pltpu.SemaphoreType.DMA((3, PIECES))],
+        name="finish",
+    )(*(pltpu.with_memory_space_constraint(v, pltpu.VMEM) for v in kept))
 
 
 def solution(mesh):

time: 51.6 us -> 44.7 us (0.87)
  other arithmetic: 3.18 us -> 0 us
  Pallas kernels: 46.6 us -> 43.9 us
  local copies, waits for them, and re-layouts: 0.89 us -> 0 us
    add x1 -> x0, other arithmetic: 3.18 us -> none  [per_device(): return (step * field, residual, residual + beta * field)]
    pallas_call x1 -> x2, Pallas kernels: 46.6 us -> 43.9 us  [the longest x1 42 us: per_device(): pl.pallas_call(lambda *refs: kernel(tiles, *refs), out_shape=(whole, whol...]
    slice x1 -> x0, local copies, waits for them, and re-layouts: 0.88 us -> none  [per_device(): step, beta = (step[:, :1], beta[:, :1])]
where the time goes in v2:
time: 44.7 us; the launch traced here: 44.5 us
  Pallas kernels  43.9 us (98%)
  between operations  0.64 us (1%)
    pallas_call x1, Pallas kernels, per_device(): pl.pallas_call(lambda *refs: kernel(tiles, *refs), out_shape=(whole, whol...  42 us
    pallas_call x1, Pallas kernels, per_device(): pl.pallas_call(finish, out_shape=(jax.ShapeDtypeStruct((n, points), f32),...  1.85 us

profile of v2, /device:TPU:1, one launch (start us, length us, event | category | flops | bytes accessed | tf_op | source)
XLA Modules:
  0.0 44.5 jit_solution(10673422539196603932)
XLA Ops:
  0.6 42.0 %iterate.1 = (f32[64,4096]{1,0:T(8,128)S(1)}, f32[64,4096]{1,0:T(8,128)S(1)}, f32[64,128]{1,0:T(8,128)S(1)}, f32[64,128]{1,0:T(8,128)S(1)}) custom-call(f32[2,4096]{1,0:T(2,128)} %refs_0_.1, f32[64,4096]{1,0:T(8,128)} %refs_1_.1), custom_call_target="tpu_custom_call" | custom-call | tf_op jit(solution)/shard_map/iterate/pallas_call | solution.py:343
  42.7 1.9 %finish.1 = (f32[64,4096]{1,0:T(8,128)}, f32[64,4096]{1,0:T(8,128)}, f32[64,4096]{1,0:T(8,128)}) custom-call(f32[64,4096]{1,0:T(8,128)S(1)} %get-tuple-element.7.field_ref, f32[64,4096]{1,0:T(8,128)S(1)} %get-tuple-element.8.image_ref, f32[64,128]{1,0:T(8,128)S(1)} %get-tuple-element.9.step_ref, f32[64,128]{1,0:T(8,128)S(1)} %get-tuple-element.10.beta_ref), custom_call_target="tpu_custom_call" | custom-call | tf_op jit(solution)/shard_map/finish/pallas_call | solution.py:370

commit v3 on v2

--- a/solution.py
+++ b/solution.py
@@ -17,7 +17,7 @@
 PLANE = NX * NY * NC
 PIECES = 4
 GROUP = 4
-EARLY = 8
+EARLY = 4
 
 f32 = jnp.float32
 bf16 = jnp.bfloat16
@@ -63,17 +63,32 @@
             col[d, h * LANE : (h + 1) * LANE, :] = jnp.broadcast_to(row, (LANE, LANE)).T
 
 
-def block(cw, col, tile, b):
-    out = []
-    for j in (2 * b, 2 * b + 1):
-        xr = cw[0:1, lanes(tile * 2 + j)]
-        yr = cw[1:2, lanes(tile * 2 + j)]
-        parts = []
-        for g in range(0, TILE, CHUNK):
+def part(cw, col, tile, j, halves):
+    xr = cw[0:1, lanes(tile * 2 + j)]
+    yr = cw[1:2, lanes(tile * 2 + j)]
+    parts = []
+    for h in halves:
+        for g in range(h * LANE, (h + 1) * LANE, CHUNK):
             rows = slice(g, g + CHUNK)
             parts.append(split(covariance(col[0, rows, :], col[1, rows, :], xr, yr)))
-        out.append([jnp.concatenate([p[i] for p in parts], 0) for i in (0, 1)])
-    return [jnp.concatenate([out[0][i], out[1][i]], 1) for i in (0, 1)]
+    return [jnp.concatenate([p[i] for p in parts], 0) for i in (0, 1)]
+
+
+def block(cw, col, tile, b):
+    left, right = [part(cw, col, tile, 2 * b + j, (0, 1)) for j in (0, 1)]
+    return [jnp.concatenate([left[i], right[i]], 1) for i in (0, 1)]
+
+
+def diagonal(cw, col, f2, acc, tile):
+    first = part(cw, col, tile, 0, (0,))
+    upper = part(cw, col, tile, 1, (0,))
+    last = part(cw, col, tile, 1, (1,))
+    values = [f2[tile * 2 + j] for j in range(2)]
+    values = jnp.concatenate(values + values, 1)
+    rows = [jnp.concatenate([first[i], upper[i]], 1) for i in (0, 1)]
+    cols = [jnp.concatenate([upper[i], last[i]], 0) for i in (0, 1)]
+    acc[:, lanes(tile * 2)] += both(dot(values, jnp.concatenate(rows, 1), NT))
+    acc[:, lanes(tile * 2 + 1)] += both(dot(values, jnp.concatenate(cols, 0), NN))
 
 
 def both(v):
@@ -115,7 +130,7 @@
     halo_c,
     halo_f,
     back,
-    part,
+    mine_ref,
     slots1,
     total1,
     slots2,
@@ -134,10 +149,15 @@
     right, left = (me + 1) % count, (me + count - 1) % count
     other = 1 - c
 
-    load_f = pltpu.make_async_copy(f_hbm, fw, load_sem.at[0])
-    load_c = pltpu.make_async_copy(c_hbm, cw.at[:, 0:points], load_sem.at[1])
+    load_c = pltpu.make_async_copy(c_hbm, cw.at[:, 0:points], load_sem.at[0])
     load_c.start()
-    load_f.start()
+    first = (GROUP + BAND) * TILE
+    spans = ((0, first), (first, points))
+    load_f = []
+    for i, (begin, end) in enumerate(spans):
+        at = slice(begin, end)
+        load_f.append(pltpu.make_async_copy(f_hbm.at[:, at], fw.at[:, at], load_sem.at[1 + i]))
+        load_f[-1].start()
 
     near = [left, right, device(y, z, x, other)]
     for dy, dz, dx in ((0, 0, 1), (0, 0, -1), (0, 1, 0), (0, -1, 0), (1, 0, 0), (-1, 0, 0)):
@@ -193,12 +213,17 @@
     cw[:, 0:points] = cw[:, 0:points] * 4.0
     columns_of(cw, col0, 0)
     cols = (col0, col1)
-    load_f.wait()
-    for j in range(points // LANE):
-        high, low = split(fw[:, j * LANE : (j + 1) * LANE])
-        f2[j, 0:n, :] = high
-        f2[j, n : 2 * n, :] = low
     wait_near()
+
+    def take(span):
+        begin, end = spans[span]
+        load_f[span].wait()
+        for j in range(begin // LANE, end // LANE):
+            high, low = split(fw[:, j * LANE : (j + 1) * LANE])
+            f2[j, 0:n, :] = high
+            f2[j, n : 2 * n, :] = low
+
+    take(0)
 
     late = tiles - BAND
 
@@ -208,11 +233,11 @@
     def _(i):
         @pl.when(i == 1)
         def _():
+            take(1)
             wait_two()
 
         @pl.when(i == EARLY // GROUP)
         def _():
-            wait_four()
             for copy in halo_copies:
                 copy.wait()
             cw[:, points : points + rim] = halo_c[...] * 4.0
@@ -224,18 +249,19 @@
         @pl.when(i == (EARLY + BAND) // GROUP)
         def _():
             back_copy.start()
-            wait_eight()
+            wait_four()
 
         places = [order(jnp.minimum(i * GROUP + k, last), late) for k in range(GROUP + 1)]
         for g in range(GROUP):
             now, following = places[g], places[g + 1]
-            for b in range(BAND + 1):
+            for b in (*range(1, BAND + 1), 0):
+                if b == 0:
+                    diagonal(cw, cols[g % 2], f2, acc, now)
+                    columns_of(cw, cols[(g + 1) % 2], following)
+                    continue
                 blocks = block(cw, cols[g % 2], now, b)
                 row_apply(f2, acc, blocks, now, b)
-                if b == 0:
-                    columns_of(cw, cols[(g + 1) % 2], following)
-                else:
-                    col_apply(f2, acc, blocks, now, b)
+                col_apply(f2, acc, blocks, now, b)
 
     sums = [jnp.zeros((n, LANE), f32) for _ in range(3)]
     for j in [*range(rim // LANE, points // LANE), *range(rim // LANE)]:
@@ -294,10 +320,11 @@
         if (dy, dx, core) != (0, 0, 0):
             at = ((y + dy) % NY, (x + dx) % NX, (c + core) % NC)
             plane.append(((at[0] * NX + at[1]) * NC + at[2], device(at[0], z, at[1], at[2])))
-    total = gather_sum(mine, part, slots1, in_plane, plane, 3)
+    total = gather_sum(mine, mine_ref, slots1, in_plane, plane, 3)
     line = []
     for k in sorted(range(1, NZ), key=lambda k: -min(k, NZ - k)):
         line.append(((z + k) % NZ, device(y, z + k, x, c)))
+    wait_eight()
     total = gather_sum(total, total1, slots2, z, line, 4)
 
     def columns(row):
@@ -358,7 +385,7 @@
             pltpu.VMEM((PLANE, 2, LANE), f32),
             pltpu.VMEM((2, LANE), f32),
             pltpu.VMEM((NZ, 2, LANE), f32),
-            pltpu.SemaphoreType.DMA((2,)),
+            pltpu.SemaphoreType.DMA((3,)),
             pltpu.SemaphoreType.DMA((5,)),
             pltpu.SemaphoreType.DMA((5,)),
             pltpu.SemaphoreType.REGULAR,

time: 44.7 us -> 45 us (level)
  no operation moved by 1% of the time
where the time goes in v3:
time: 45 us; the launch traced here: 44.9 us
  Pallas kernels  44.2 us (98%)
  between operations  0.64 us (1%)
    pallas_call x1, Pallas kernels, per_device(): pl.pallas_call(lambda *refs: kernel(tiles, *refs), out_shape=(whole, whol...  42.4 us
    pallas_call x1, Pallas kernels, per_device(): pl.pallas_call(finish, out_shape=(jax.ShapeDtypeStruct((n, points), f32),...  1.85 us

profile of v3, /device:TPU:1, one launch (start us, length us, event | category | flops | bytes accessed | tf_op | source)
XLA Modules:
  0.0 44.9 jit_solution(16474201787785413629)
XLA Ops:
  0.6 42.4 %iterate.1 = (f32[64,4096]{1,0:T(8,128)S(1)}, f32[64,4096]{1,0:T(8,128)S(1)}, f32[64,128]{1,0:T(8,128)S(1)}, f32[64,128]{1,0:T(8,128)S(1)}) custom-call(f32[2,4096]{1,0:T(2,128)} %refs_0_.1, f32[64,4096]{1,0:T(8,128)} %refs_1_.1), custom_call_target="tpu_custom_call" | custom-call | tf_op jit(solution)/shard_map/iterate/pallas_call | solution.py:370
  43.0 1.9 %finish.1 = (f32[64,4096]{1,0:T(8,128)}, f32[64,4096]{1,0:T(8,128)}, f32[64,4096]{1,0:T(8,128)}) custom-call(f32[64,4096]{1,0:T(8,128)S(1)} %get-tuple-element.7.field_ref, f32[64,4096]{1,0:T(8,128)S(1)} %get-tuple-element.8.image_ref, f32[64,128]{1,0:T(8,128)S(1)} %get-tuple-element.9.step_ref, f32[64,128]{1,0:T(8,128)S(1)} %get-tuple-element.10.beta_ref), custom_call_target="tpu_custom_call" | custom-call | tf_op jit(solution)/shard_map/finish/pallas_call | solution.py:397

commit v4 on v3

--- a/solution.py
+++ b/solution.py
@@ -17,7 +17,8 @@
 PLANE = NX * NY * NC
 PIECES = 4
 GROUP = 4
-EARLY = 4
+ENDS = 2
+EARLY = 6
 
 f32 = jnp.float32
 bf16 = jnp.bfloat16
@@ -151,7 +152,7 @@
 
     load_c = pltpu.make_async_copy(c_hbm, cw.at[:, 0:points], load_sem.at[0])
     load_c.start()
-    first = (GROUP + BAND) * TILE
+    first = (ENDS + BAND) * TILE
     spans = ((0, first), (first, points))
     load_f = []
     for i, (begin, end) in enumerate(spans):
@@ -229,30 +230,9 @@
 
     last = tiles - 1
 
-    @pl.loop(0, tiles // GROUP)
-    def _(i):
-        @pl.when(i == 1)
-        def _():
-            take(1)
-            wait_two()
-
-        @pl.when(i == EARLY // GROUP)
-        def _():
-            for copy in halo_copies:
-                copy.wait()
-            cw[:, points : points + rim] = halo_c[...] * 4.0
-            for j in range(rim // LANE):
-                high, low = split(halo_f[:, j * LANE : (j + 1) * LANE])
-                f2[points // LANE + j, 0:n, :] = high
-                f2[points // LANE + j, n : 2 * n, :] = low
-
-        @pl.when(i == (EARLY + BAND) // GROUP)
-        def _():
-            back_copy.start()
-            wait_four()
-
-        places = [order(jnp.minimum(i * GROUP + k, last), late) for k in range(GROUP + 1)]
-        for g in range(GROUP):
+    def strips(start, number):
+        places = [order(jnp.minimum(start + k, last), late) for k in range(number + 1)]
+        for g in range(number):
             now, following = places[g], places[g + 1]
             for b in (*range(1, BAND + 1), 0):
                 if b == 0:
@@ -263,6 +243,35 @@
                 row_apply(f2, acc, blocks, now, b)
                 col_apply(f2, acc, blocks, now, b)
 
+    strips(0, ENDS)
+
+    @pl.loop(0, (tiles - 2 * ENDS) // GROUP)
+    def _(i):
+        start = ENDS + i * GROUP
+
+        @pl.when(start == ENDS)
+        def _():
+            take(1)
+            wait_two()
+
+        @pl.when(start == EARLY)
+        def _():
+            for copy in halo_copies:
+                copy.wait()
+            cw[:, points : points + rim] = halo_c[...] * 4.0
+            for j in range(rim // LANE):
+                high, low = split(halo_f[:, j * LANE : (j + 1) * LANE])
+                f2[points // LANE + j, 0:n, :] = high
+                f2[points // LANE + j, n : 2 * n, :] = low
+
+        @pl.when(start == EARLY + BAND)
+        def _():
+            back_copy.start()
+            wait_four()
+
+        strips(start, GROUP)
+
+    strips(tiles - ENDS, ENDS)
     sums = [jnp.zeros((n, LANE), f32) for _ in range(3)]
     for j in [*range(rim // LANE, points // LANE), *range(rim // LANE)]:
         if j == 0:

time: 45 us -> 44.1 us (0.980)
  Pallas kernels: 44.2 us -> 43.3 us
    pallas_call x1, Pallas kernels: 42.4 us -> 41.5 us  [per_device(): pl.pallas_call(lambda *refs: kernel(tiles, *refs), out_shape=(whole, whol...]
where the time goes in v4:
time: 44.1 us; the launch traced here: 44 us
  Pallas kernels  43.3 us (98%)
  between operations  0.64 us (1%)
    pallas_call x1, Pallas kernels, per_device(): pl.pallas_call(lambda *refs: kernel(tiles, *refs), out_shape=(whole, whol...  41.5 us
    pallas_call x1, Pallas kernels, per_device(): pl.pallas_call(finish, out_shape=(jax.ShapeDtypeStruct((n, points), f32),...  1.85 us

profile of v4, /device:TPU:1, one launch (start us, length us, event | category | flops | bytes accessed | tf_op | source)
XLA Modules:
  0.0 44.0 jit_solution(17972441053741235354)
XLA Ops:
  0.6 41.5 %iterate.1 = (f32[64,4096]{1,0:T(8,128)S(1)}, f32[64,4096]{1,0:T(8,128)S(1)}, f32[64,128]{1,0:T(8,128)S(1)}, f32[64,128]{1,0:T(8,128)S(1)}) custom-call(f32[2,4096]{1,0:T(2,128)} %refs_0_.1, f32[64,4096]{1,0:T(8,128)} %refs_1_.1), custom_call_target="tpu_custom_call" | custom-call | tf_op jit(solution)/shard_map/iterate/pallas_call | solution.py:379
  42.1 1.9 %finish.1 = (f32[64,4096]{1,0:T(8,128)}, f32[64,4096]{1,0:T(8,128)}, f32[64,4096]{1,0:T(8,128)}) custom-call(f32[64,4096]{1,0:T(8,128)S(1)} %get-tuple-element.7.field_ref, f32[64,4096]{1,0:T(8,128)S(1)} %get-tuple-element.8.image_ref, f32[64,128]{1,0:T(8,128)S(1)} %get-tuple-element.9.step_ref, f32[64,128]{1,0:T(8,128)S(1)} %get-tuple-element.10.beta_ref), custom_call_target="tpu_custom_call" | custom-call | tf_op jit(solution)/shard_map/finish/pallas_call | solution.py:406

commit v5 on v4

--- a/solution.py
+++ b/solution.py
@@ -214,8 +214,6 @@
     cw[:, 0:points] = cw[:, 0:points] * 4.0
     columns_of(cw, col0, 0)
     cols = (col0, col1)
-    wait_near()
-
     def take(span):
         begin, end = spans[span]
         load_f[span].wait()
@@ -230,20 +228,22 @@
 
     last = tiles - 1
 
-    def strips(start, number):
+    def strips(start, number, odd=0):
         places = [order(jnp.minimum(start + k, last), late) for k in range(number + 1)]
         for g in range(number):
             now, following = places[g], places[g + 1]
             for b in (*range(1, BAND + 1), 0):
                 if b == 0:
-                    diagonal(cw, cols[g % 2], f2, acc, now)
-                    columns_of(cw, cols[(g + 1) % 2], following)
+                    diagonal(cw, cols[(odd + g) % 2], f2, acc, now)
+                    columns_of(cw, cols[(odd + g + 1) % 2], following)
                     continue
-                blocks = block(cw, cols[g % 2], now, b)
+                blocks = block(cw, cols[(odd + g) % 2], now, b)
                 row_apply(f2, acc, blocks, now, b)
                 col_apply(f2, acc, blocks, now, b)
 
-    strips(0, ENDS)
+    strips(0, 1)
+    wait_near()
+    strips(1, ENDS - 1, 1)
 
     @pl.loop(0, (tiles - 2 * ENDS) // GROUP)
     def _(i):
@@ -252,10 +252,10 @@
         @pl.when(start == ENDS)
         def _():
             take(1)
-            wait_two()
 
         @pl.when(start == EARLY)
         def _():
+            wait_two()
             for copy in halo_copies:
                 copy.wait()
             cw[:, points : points + rim] = halo_c[...] * 4.0

time: 44.1 us -> 44.1 us (level)
  no operation moved by 1% of the time
where the time goes in v5:
time: 44.1 us; the launch traced here: 44 us
  Pallas kernels  43.3 us (98%)
  between operations  0.64 us (1%)
    pallas_call x1, Pallas kernels, per_device(): pl.pallas_call(lambda *refs: kernel(tiles, *refs), out_shape=(whole, whol...  41.5 us
    pallas_call x1, Pallas kernels, per_device(): pl.pallas_call(finish, out_shape=(jax.ShapeDtypeStruct((n, points), f32),...  1.85 us

profile of v5, /device:TPU:1, one launch (start us, length us, event | category | flops | bytes accessed | tf_op | source)
XLA Modules:
  0.0 44.0 jit_solution(9260947686998456399)
XLA Ops:
  0.6 41.5 %iterate.1 = (f32[64,4096]{1,0:T(8,128)S(1)}, f32[64,4096]{1,0:T(8,128)S(1)}, f32[64,128]{1,0:T(8,128)S(1)}, f32[64,128]{1,0:T(8,128)S(1)}) custom-call(f32[2,4096]{1,0:T(2,128)} %refs_0_.1, f32[64,4096]{1,0:T(8,128)} %refs_1_.1), custom_call_target="tpu_custom_call" | custom-call | tf_op jit(solution)/shard_map/iterate/pallas_call | solution.py:379
  42.1 1.9 %finish.1 = (f32[64,4096]{1,0:T(8,128)}, f32[64,4096]{1,0:T(8,128)}, f32[64,4096]{1,0:T(8,128)}) custom-call(f32[64,4096]{1,0:T(8,128)S(1)} %get-tuple-element.7.field_ref, f32[64,4096]{1,0:T(8,128)S(1)} %get-tuple-element.8.image_ref, f32[64,128]{1,0:T(8,128)S(1)} %get-tuple-element.9.step_ref, f32[64,128]{1,0:T(8,128)S(1)} %get-tuple-element.10.beta_ref), custom_call_target="tpu_custom_call" | custom-call | tf_op jit(solution)/shard_map/finish/pallas_call | solution.py:406

commit v6 on v5

--- a/solution.py
+++ b/solution.py
@@ -17,8 +17,8 @@
 PLANE = NX * NY * NC
 PIECES = 4
 GROUP = 4
-ENDS = 2
-EARLY = 6
+FIRST = 3
+EARLY = 7
 
 f32 = jnp.float32
 bf16 = jnp.bfloat16
@@ -152,7 +152,7 @@
 
     load_c = pltpu.make_async_copy(c_hbm, cw.at[:, 0:points], load_sem.at[0])
     load_c.start()
-    first = (ENDS + BAND) * TILE
+    first = (FIRST + BAND) * TILE
     spans = ((0, first), (first, points))
     load_f = []
     for i, (begin, end) in enumerate(spans):
@@ -243,13 +243,15 @@
 
     strips(0, 1)
     wait_near()
-    strips(1, ENDS - 1, 1)
-
-    @pl.loop(0, (tiles - 2 * ENDS) // GROUP)
+    strips(1, FIRST - 1, 1)
+    passes = (tiles - FIRST) // GROUP
+    rest = tiles - FIRST - passes * GROUP
+
+    @pl.loop(0, passes)
     def _(i):
-        start = ENDS + i * GROUP
-
-        @pl.when(start == ENDS)
+        start = FIRST + i * GROUP
+
+        @pl.when(i == 0)
         def _():
             take(1)
 
@@ -269,9 +271,9 @@
             back_copy.start()
             wait_four()
 
-        strips(start, GROUP)
-
-    strips(tiles - ENDS, ENDS)
+        strips(start, GROUP, FIRST % 2)
+
+    strips(tiles - rest, rest, (tiles - rest) % 2)
     sums = [jnp.zeros((n, LANE), f32) for _ in range(3)]
     for j in [*range(rim // LANE, points // LANE), *range(rim // LANE)]:
         if j == 0:

time: 44.1 us -> 44.1 us (level)
  no operation moved by 1% of the time
where the time goes in v6:
time: 44.1 us; the launch traced here: 44 us
  Pallas kernels  43.3 us (98%)
  between operations  0.64 us (1%)
    pallas_call x1, Pallas kernels, per_device(): pl.pallas_call(lambda *refs: kernel(tiles, *refs), out_shape=(whole, whol...  41.5 us
    pallas_call x1, Pallas kernels, per_device(): pl.pallas_call(finish, out_shape=(jax.ShapeDtypeStruct((n, points), f32),...  1.85 us

profile of v6, /device:TPU:1, one launch (start us, length us, event | category | flops | bytes accessed | tf_op | source)
XLA Modules:
  0.0 44.0 jit_solution(5976303430518287297)
XLA Ops:
  0.6 41.5 %iterate.1 = (f32[64,4096]{1,0:T(8,128)S(1)}, f32[64,4096]{1,0:T(8,128)S(1)}, f32[64,128]{1,0:T(8,128)S(1)}, f32[64,128]{1,0:T(8,128)S(1)}) custom-call(f32[2,4096]{1,0:T(2,128)} %refs_0_.1, f32[64,4096]{1,0:T(8,128)} %refs_1_.1), custom_call_target="tpu_custom_call" | custom-call | tf_op jit(solution)/shard_map/iterate/pallas_call | solution.py:381
  42.1 1.9 %finish.1 = (f32[64,4096]{1,0:T(8,128)}, f32[64,4096]{1,0:T(8,128)}, f32[64,4096]{1,0:T(8,128)}) custom-call(f32[64,4096]{1,0:T(8,128)S(1)} %get-tuple-element.7.field_ref, f32[64,4096]{1,0:T(8,128)S(1)} %get-tuple-element.8.image_ref, f32[64,128]{1,0:T(8,128)S(1)} %get-tuple-element.9.step_ref, f32[64,128]{1,0:T(8,128)S(1)} %get-tuple-element.10.beta_ref), custom_call_target="tpu_custom_call" | custom-call | tf_op jit(solution)/shard_map/finish/pallas_call | solution.py:408

commit v7 on v6

--- a/solution.py
+++ b/solution.py
@@ -18,7 +18,6 @@
 PIECES = 4
 GROUP = 4
 FIRST = 3
-EARLY = 7
 
 f32 = jnp.float32
 bf16 = jnp.bfloat16
@@ -107,12 +106,6 @@
     values = [f2[tile * 2 + j] for j in range(2)]
     out = dot(jnp.concatenate(values + values, 1), jnp.concatenate(blocks, 0), NN)
     acc[:, lanes((tile + b) * 2, 2)] += both(out)
-
-
-def order(step, late):
-    return jnp.where(
-        step < EARLY, step, jnp.where(step < EARLY + BAND, step + late - EARLY, step - BAND)
-    )
 
 
 def kernel(
@@ -131,6 +124,7 @@
     halo_c,
     halo_f,
     back,
+    kept,
     mine_ref,
     slots1,
     total1,
@@ -226,11 +220,9 @@
 
     late = tiles - BAND
 
-    last = tiles - 1
-
-    def strips(start, number, odd=0):
-        places = [order(jnp.minimum(start + k, last), late) for k in range(number + 1)]
-        for g in range(number):
+
+    def strips(places, odd=0, over=None):
+        for g in range(len(places) - 1):
             now, following = places[g], places[g + 1]
             for b in (*range(1, BAND + 1), 0):
                 if b == 0:
@@ -238,42 +230,48 @@
                     columns_of(cw, cols[(odd + g + 1) % 2], following)
                     continue
                 blocks = block(cw, cols[(odd + g) % 2], now, b)
-                row_apply(f2, acc, blocks, now, b)
+                if over is not None and now + b >= tiles:
+                    for i in (0, 1):
+                        for h in (0, 1):
+                            kept[len(over), i, h, :, :] = blocks[i][:, h * LANE : (h + 1) * LANE]
+                    over.append((now, b))
+                else:
+                    row_apply(f2, acc, blocks, now, b)
                 col_apply(f2, acc, blocks, now, b)
 
-    strips(0, 1)
+    strips([0, 1])
     wait_near()
-    strips(1, FIRST - 1, 1)
-    passes = (tiles - FIRST) // GROUP
-    rest = tiles - FIRST - passes * GROUP
-
-    @pl.loop(0, passes)
+    take(1)
+    strips([1, 2, late], 1)
+    halo_copies[0].wait()
+    cw[:, points : points + rim] = halo_c[...] * 4.0
+    over = []
+    strips([*range(late, tiles), FIRST], FIRST % 2, over)
+    back_copy.start()
+
+    @pl.loop(0, (late - FIRST) // GROUP)
     def _(i):
-        start = FIRST + i * GROUP
-
         @pl.when(i == 0)
         def _():
-            take(1)
-
-        @pl.when(start == EARLY)
+            wait_two()
+
+        @pl.when(i == 1)
         def _():
-            wait_two()
-            for copy in halo_copies:
-                copy.wait()
-            cw[:, points : points + rim] = halo_c[...] * 4.0
-            for j in range(rim // LANE):
-                high, low = split(halo_f[:, j * LANE : (j + 1) * LANE])
-                f2[points // LANE + j, 0:n, :] = high
-                f2[points // LANE + j, n : 2 * n, :] = low
-
-        @pl.when(start == EARLY + BAND)
-        def _():
-            back_copy.start()
             wait_four()
 
-        strips(start, GROUP, FIRST % 2)
-
-    strips(tiles - rest, rest, (tiles - rest) % 2)
+        start = FIRST + i * GROUP
+        strips([start + k for k in range(GROUP + 1)], (FIRST + BAND) % 2)
+
+    halo_copies[1].wait()
+    for j in range(rim // LANE):
+        high, low = split(halo_f[:, j * LANE : (j + 1) * LANE])
+        f2[points // LANE + j, 0:n, :] = high
+        f2[points // LANE + j, n : 2 * n, :] = low
+    for k, (tile, b) in enumerate(over):
+        row_apply(f2, acc, [jnp.concatenate([kept[k, i, 0], kept[k, i, 1]], 1) for i in (0, 1)], tile, b)
+    rest = (late - FIRST) % GROUP
+    strips(list(range(late - rest, late + 1)), (FIRST + BAND) % 2)
+
     sums = [jnp.zeros((n, LANE), f32) for _ in range(3)]
     for j in [*range(rim // LANE, points // LANE), *range(rim // LANE)]:
         if j == 0:
@@ -392,6 +390,7 @@
             pltpu.VMEM((2, rim), f32),
             pltpu.VMEM((n, rim), f32),
             pltpu.VMEM((n, rim), f32),
+            pltpu.VMEM((BAND * (BAND + 1) // 2, 2, 2, TILE, LANE), bf16),
             pltpu.VMEM((2, LANE), f32),
             pltpu.VMEM((PLANE, 2, LANE), f32),
             pltpu.VMEM((2, LANE), f32),

time: 44.1 us -> 43.9 us (level)
  no operation moved by 1% of the time
where the time goes in v7:
time: 43.9 us; the launch traced here: 43.8 us
  Pallas kernels  43 us (98%)
  between operations  0.8 us (2%)
    pallas_call x1, Pallas kernels, per_device(): pl.pallas_call(lambda *refs: kernel(tiles, *refs), out_shape=(whole, whol...  41.1 us
    pallas_call x1, Pallas kernels, per_device(): pl.pallas_call(finish, out_shape=(jax.ShapeDtypeStruct((n, points), f32),...  1.85 us

profile of v7, /device:TPU:1, one launch (start us, length us, event | category | flops | bytes accessed | tf_op | source)
XLA Modules:
  0.0 43.8 jit_solution(186168376409989630)
XLA Ops:
  0.6 41.1 %iterate.1 = (f32[64,4096]{1,0:T(8,128)S(1)}, f32[64,4096]{1,0:T(8,128)S(1)}, f32[64,128]{1,0:T(8,128)S(1)}, f32[64,128]{1,0:T(8,128)S(1)}) custom-call(f32[2,4096]{1,0:T(2,128)} %refs_0_.1, f32[64,4096]{1,0:T(8,128)} %refs_1_.1), custom_call_target="tpu_custom_call" | custom-call | tf_op jit(solution)/shard_map/iterate/pallas_call | solution.py:379
  41.7 1.9 %finish.1 = (f32[64,4096]{1,0:T(8,128)}, f32[64,4096]{1,0:T(8,128)}, f32[64,4096]{1,0:T(8,128)}) custom-call(f32[64,4096]{1,0:T(8,128)S(1)} %get-tuple-element.7.field_ref, f32[64,4096]{1,0:T(8,128)S(1)} %get-tuple-element.8.image_ref, f32[64,128]{1,0:T(8,128)S(1)} %get-tuple-element.9.step_ref, f32[64,128]{1,0:T(8,128)S(1)} %get-tuple-element.10.beta_ref), custom_call_target="tpu_custom_call" | custom-call | tf_op jit(solution)/shard_map/finish/pallas_call | solution.py:407
